TPU v7x, 32 devices: a whole 2x2x4 slice. The times are simulated.
32 devices in a mesh: ctx: 8 (over z, y), tp: 4 (over x, core).
Axes of the slice: x: 2, y: 2, z: 4, core: 2. Of those that a mesh axis runs over, the one named last changes fastest.
Arguments:
- tokens: bfloat16 [4096, 5376], P(('ctx', 'tp')), may hold values from -8 to 8
- positions: int32 [4096], replicated, may hold values from 0 to 16383, as said below
- w_query: bfloat16 [5376, 2048], P('ctx', 'tp'), may hold values from -1 to 1
- key_matrix: bfloat16 [5376, 1024], P('ctx', 'tp'), may hold values from -1 to 1
- value_matrix: bfloat16 [5376, 1024], P('ctx', 'tp'), may hold values from -0.078125 to 0.078125
- w_out: bfloat16 [2048, 5376], P('tp', 'ctx'), may hold values from -0.125 to 0.125
- gain_in: float32 [5376], replicated, may hold values from 0.1 to 1.9
- gain_query: float32 [128], replicated, may hold values from 0.5 to 14
- gain_key: float32 [128], replicated, may hold values from 0.5 to 14
- gain_post: float32 [5376], replicated, may hold values from 0.1 to 1.9
Outputs:
- layer_out: bfloat16 [4096, 5376], P(('ctx', 'tp'))
Inputs may be any that keep to these rules, and one draw needn't show every extreme that they name: (positions) rise strictly along the tokens, by 1 to 4 from one token to the next, and the last token stands at 16383.
All inputs are finite; a program needn't handle non-finite values.
Results may differ from a plain program's by a relative error of at most 0.013.
The roundings to bfloat16 on the way count: a program that leaves them out, or rounds other values in their place, can miss the bound.
Values may be sent and summed in bfloat16 or wider, within the bound.
A program may use at most 128 MiB of HBM per device.

v0:
```python
import jax
import jax.numpy as jnp
from jax import lax
from jax.sharding import PartitionSpec as P

HEAD_SIZE = 128
QS = 168
LOOKBACK_WINDOW = 1024
EPSILON = 1e-06
ROPE_BASE = 10000.0


def shifted(value, axis, steps):
    count = lax.axis_size(axis)
    leading, last = (max(0, -steps), min(count, count - steps))
    return lax.ppermute(value, axis, [(source, source + steps) for source in range(leading, last)])


def row_norm(values, scales):
    mean_square = jnp.mean(values * values, axis=-1, keepdims=True)
    return values * lax.rsqrt(mean_square + EPSILON) * scales


def rotate(head_rows, offsets):
    half_dim = head_rows.shape[-1] // 2
    frequency = ROPE_BASE ** (
        -(jnp.arange(half_dim, dtype=jnp.float32) * 2.0) / head_rows.shape[-1]
    )
    angles = offsets.astype(jnp.float32)[:, None] * frequency[None, :]
    cosine = jnp.cos(angles)[:, None, :]
    sine_wave = jnp.sin(angles)[:, None, :]
    first_half = head_rows[..., :half_dim]
    second_half = head_rows[..., half_dim:]
    return jnp.concatenate(
        [
            first_half * cosine - second_half * sine_wave,
            second_half * cosine + first_half * sine_wave,
        ],
        axis=-1,
    )


def attend(query_matrix, projected_keys, projected_values, query_offsets, key_offsets, key_valid):
    scores = jnp.einsum(
        "qkgd,skd->kgqs", query_matrix, projected_keys, preferred_element_type=jnp.float32
    ) * QS ** (-0.5)
    position_gap = query_offsets[:, None] - key_offsets[None, :]
    allowed = key_valid[None, :] & (position_gap >= 0) & (position_gap < LOOKBACK_WINDOW)
    scores = jnp.where(allowed[None, None], scores, -1e30)
    row_max = jnp.max(scores, axis=-1, keepdims=True)
    weights = jnp.where(allowed[None, None], jnp.exp(scores - row_max), 0.0)
    totals = jnp.sum(weights, axis=-1, keepdims=True)
    rounded = weights.astype(jnp.bfloat16)
    mixed = jnp.einsum(
        "kgqs,skd->qkgd", rounded, projected_values, preferred_element_type=jnp.float32
    )
    mixed = mixed / jnp.transpose(totals, (2, 0, 1, 3))
    return mixed.astype(jnp.bfloat16).reshape(query_matrix.shape[0], -1)


def shards(
    tokens,
    positions,
    w_query,
    key_matrix,
    value_matrix,
    w_out,
    gain_in,
    gain_query,
    gain_key,
    gain_post,
):
    gathered = lax.all_gather(tokens, "tp", axis=0, tiled=True)
    normalized_rows = row_norm(gathered.astype(jnp.float32), gain_in).astype(jnp.bfloat16)
    row_count = normalized_rows.shape[0]
    block_start = lax.axis_index("ctx") * row_count
    offsets_all = positions - positions[0]
    query_offsets = lax.dynamic_slice_in_dim(offsets_all, block_start, row_count, 0)

    def add_rows(weight_rows):
        return jnp.dot(normalized_rows, weight_rows, preferred_element_type=jnp.float32)

    query_raw = add_rows(lax.all_gather(w_query, "ctx", axis=0, tiled=True))
    unnormed_keys = add_rows(lax.all_gather(key_matrix, "ctx", axis=0, tiled=True))
    value_raw = add_rows(lax.all_gather(value_matrix, "ctx", axis=0, tiled=True))
    key_heads = key_matrix.shape[1] // HEAD_SIZE
    projected_keys = rotate(
        row_norm(unnormed_keys.reshape(row_count, key_heads, HEAD_SIZE), gain_key), query_offsets
    ).astype(jnp.bfloat16)
    projected_values = value_raw.astype(jnp.bfloat16).reshape(row_count, key_heads, HEAD_SIZE)
    own_pair = jnp.stack([projected_keys, projected_values])
    window_blocks = LOOKBACK_WINDOW // row_count
    earlier = []
    carried = own_pair
    for relay_step in range(window_blocks):
        carried = shifted(carried, "ctx", 1)
        earlier.insert(0, carried)
    window_pair = jnp.concatenate(earlier + [own_pair], axis=1)
    query_heads = w_query.shape[1] // HEAD_SIZE
    query_matrix = rotate(
        row_norm(query_raw.reshape(row_count, query_heads, HEAD_SIZE), gain_query), query_offsets
    ).astype(jnp.bfloat16)
    query_matrix = query_matrix.reshape(row_count, key_heads, query_heads // key_heads, HEAD_SIZE)
    padded_offsets = jnp.concatenate(
        [jnp.zeros((LOOKBACK_WINDOW,), jnp.int32), offsets_all], axis=0
    )
    key_offsets = lax.dynamic_slice_in_dim(
        padded_offsets, block_start, LOOKBACK_WINDOW + row_count, 0
    )
    key_valid = (
        block_start + jnp.arange(LOOKBACK_WINDOW + row_count, dtype=jnp.int32) >= LOOKBACK_WINDOW
    )
    attended = attend(
        query_matrix, window_pair[0], window_pair[1], query_offsets, key_offsets, key_valid
    )
    projected = jnp.dot(
        attended,
        lax.all_gather(w_out, "ctx", axis=1, tiled=True),
        preferred_element_type=jnp.float32,
    )
    summed = lax.psum_scatter(
        projected.astype(jnp.bfloat16), "tp", scatter_dimension=0, tiled=True
    ).astype(jnp.float32)
    return (tokens.astype(jnp.float32) + row_norm(summed, gain_post)).astype(jnp.bfloat16)


def solution(mesh):
    in_specs = (
        P(("ctx", "tp"), None),
        P(),
        P("ctx", "tp"),
        P("ctx", "tp"),
        P("ctx", "tp"),
        P("tp", "ctx"),
        P(),
        P(),
        P(),
        P(),
    )
    out_specs = P(("ctx", "tp"), None)
    return jax.shard_map(shards, mesh=mesh, in_specs=in_specs, out_specs=out_specs, check_vma=False)
```

profile of v0, /device:TPU:0, one launch (start us, length us, event | category | flops | bytes accessed | tf_op | source)
XLA Modules:
  0.0 434.3 jit_solution(12205699914672215212)
XLA Ops:
  6.5 0.0 copy-start.5
  6.5 0.0 all-gather.6.cloned.1.call-start
  6.5 0.7 all-gather.6.cloned.1.call-update
  7.3 0.0 all-gather.8.cloned.1.call-start
  7.3 0.7 all-gather.8.cloned.1.call-update
  8.0 0.0 all-gather.10.cloned.1.call-start
  8.1 0.7 all-gather.10.cloned.1.call-update
  8.7 0.0 all-gather.12.cloned.1.call-start
  8.8 0.5 all-gather.12.cloned.1.call-update
  9.3 0.0 all-gather.14.cloned.1.call-start
  9.4 0.5 all-gather.14.cloned.1.call-update
  9.9 0.0 reduce-scatter.2.cloned.1.call-start
  10.0 1.2 slice.22
  11.2 1.4 broadcast_subtract_fusion
  12.5 0.1 fusion.41
  12.6 0.5 multiply_cosine_fusion
  13.2 0.1 copy.20
  13.3 0.1 copy.21
  13.4 40.1 %all-gather.6.cloned.1.call-done = bf16[512,5376]{1,0:T(8,128)(2,1)} async-done(((bf16[128,5376]{1,0:T(8,128)(2,1)}), bf16[512,5376]{1,0:T(8,128)(2,1)}) %all-gather.6.cloned.1.call-update) | async-done | bytes 5505040 | tf_op jit(solution)/shard_map/all_gather | solution.py:73
  53.5 3.7 fusion.1
  57.3 54.5 %all-gather.8.cloned.1.call-done = bf16[5376,256]{1,0:T(8,128)(2,1)} async-done(((bf16[672,256]{1,0:T(8,128)(2,1)}), bf16[5376,256]{1,0:T(8,128)(2,1)}) %all-gather.8.cloned.1.call-update) | async-done | bytes 2752528 | tf_op jit(solution)/shard_map/all_gather | solution.py:84
  111.8 0.0 copy-done.5
  111.8 5.4 %multiply_reduce_fusion.1 = (f32[512,2]{0,1:T(2,128)S(1)}, f32[512,256]{0,1:T(8,128)S(1)}) fusion(bf16[5376,256]{1,0:T(8,128)(2,1)} %all-gather.8.cloned.1.call-done, bf16[512,5376]{1,0:T(8,128)(2,1)} %all-gather.6.cloned.1.call-done, f32[5376]{0:T(1024)S(1)} %copy-done.5, f32[512]{0:T(512)S(1)} %add_rsqrt_fusion.2), kind=kOutput, calls=%fused_computation.43 | convolution fusion | flops 1420557312 | bytes 8809472 | tf_op jit(solution)/shard_map/dot_general | solution.py:81
  117.2 0.2 copy.19
  117.4 0.0 copy-start.3
  117.4 51.2 %all-gather.10.cloned.1.call-done = bf16[5376,256]{1,0:T(8,128)(2,1)} async-done(((bf16[672,256]{1,0:T(8,128)(2,1)}), bf16[5376,256]{1,0:T(8,128)(2,1)}) %all-gather.10.cloned.1.call-update) | async-done | bytes 2752528 | tf_op jit(solution)/shard_map/all_gather | solution.py:85
  168.6 5.4 %convolution_convert_fusion.1 = bf16[512,256]{0,1:T(8,128)(2,1)S(1)} fusion(bf16[5376,256]{1,0:T(8,128)(2,1)} %all-gather.10.cloned.1.call-done, bf16[512,5376]{1,0:T(8,128)(2,1)} %all-gather.6.cloned.1.call-done, f32[5376]{0:T(1024)S(1)} %copy-done.5, f32[512]{0:T(512)S(1)} %add_rsqrt_fusion.2), kind=kOutput, calls=%fused_computation.30 | convolution fusion | flops 1420427264 | bytes 8543232 | tf_op jit(solution)/shard_map/dot_general | solution.py:81
  174.0 0.2 copy.22
  174.2 0.0 copy-done.3
  174.2 0.2 multiply_multiply_fusion.1
  174.4 0.2 fusion.28
  174.6 0.2 pad_maximum_fusion
  174.8 2.5 collective-permute-start
  177.3 0.1 pad_dynamic-slice_fusion
  177.4 16.8 %collective-permute-done = bf16[2,512,2,128]{3,1,2,0:T(8,128)(2,1)S(1)} collective-permute-done((bf16[2,512,2,128]{3,1,2,0:T(8,128)(2,1)S(1)}, bf16[2,512,2,128]{3,1,2,0:T(8,128)(2,1)S(1)}, u32[]{:S(2)}, u32[]{:S(2)}) %collective-permute-start) | collective-permute-done | bytes 524320 | tf_op jit(solution)/shard_map/ppermute | solution.py:16
  194.2 0.0 copy-start.1
  194.2 9.1 %collective-permute-start.1 = (bf16[2,512,2,128]{3,1,2,0:T(8,128)(2,1)S(1)}, bf16[2,512,2,128]{3,1,2,0:T(8,128)(2,1)S(1)}, u32[]{:S(2)}, u32[]{:S(2)}) collective-permute-start(bf16[2,512,2,128]{3,1,2,0:T(8,128)(2,1)S(1)} %collective-permute-done), channel_id=1, source_target_pairs={{0,4},{4,8},{8,12},{12,16},{16,20},{20,24},{24,28},{1,5},{5,9},{9,... | collective-permute-start | bytes 1572872 | tf_op jit(solution)/shard_map/ppermute | solution.py:16
  203.3 1.3 fusion.11
  204.5 0.0 copy-done.1
  204.5 5.2 %collective-permute-done.1 = bf16[2,512,2,128]{3,1,2,0:T(8,128)(2,1)S(1)} collective-permute-done((bf16[2,512,2,128]{3,1,2,0:T(8,128)(2,1)S(1)}, bf16[2,512,2,128]{3,1,2,0:T(8,128)(2,1)S(1)}, u32[]{:S(2)}, u32[]{:S(2)}) %collective-permute-start.1) | collective-permute-done | bytes 524320 | tf_op jit(solution)/shard_map/ppermute | solution.py:16
  209.7 1.2 maximum_maximum_fusion
  211.0 0.0 copy-start.4
  211.0 63.6 %all-gather.12.cloned.1.call-done = bf16[5376,512]{1,0:T(8,128)(2,1)} async-done(((bf16[672,512]{1,0:T(8,128)(2,1)}), bf16[5376,512]{1,0:T(8,128)(2,1)}) %all-gather.12.cloned.1.call-update) | async-done | bytes 5505040 | tf_op jit(solution)/shard_map/all_gather | solution.py:83
  274.5 8.0 %multiply_reduce_fusion = (f32[512,4]{0,1:T(4,128)S(1)}, f32[512,512]{0,1:T(8,128)S(1)}) fusion(bf16[5376,512]{1,0:T(8,128)(2,1)} %all-gather.12.cloned.1.call-done, bf16[512,5376]{1,0:T(8,128)(2,1)} %all-gather.6.cloned.1.call-done, f32[5376]{0:T(1024)S(1)} %copy-done.5, f32[512]{0:T(512)S(1)} %add_rsqrt_fusion.2), kind=kOutput, calls=%fused_computation.32 | convolution fusion | flops 2830104576 | bytes 12090368 | tf_op jit(solution)/shard_map/dot_general | solution.py:81
  282.6 0.0 copy-done.4
  282.6 0.2 multiply_multiply_fusion
  282.8 0.2 subtract_convert_fusion
  283.0 1.0 copy.23
  284.0 0.3 copy.24
  284.2 9.1 %fusion.42 = (f32[2,2,512]{2,1,0:T(2,128)S(1)}, bf16[2,2,512,1536]{2,3,1,0:T(8,128)(2,1)}) fusion(pred[512,1536]{0,1:T(8,128)(4,1)S(1)} %fusion.11, bf16[2,1536,2,128]{3,1,2,0:T(8,128)(2,1)S(1)} %maximum_maximum_fusion, bf16[512,2,2,64]{3,0,2,1:T(8,128)(2,1)S(1)} %bitcast.65, bf16[512,2,2,64]{3,0,2,1:T(8,128)(2,1)} %bitcast.64), kind=kOutput, calls=%fused_computation.63 | convolution fusion | flops 825230848 | bytes 9183232 | tf_op jit(solution)/shard_map/sub | solution.py:51
  293.3 3.9 fusion.24
  297.2 66.7 %all-gather.14.cloned.1.call-done = bf16[512,5376]{0,1:T(8,128)(2,1)} async-done(((bf16[512,672]{0,1:T(8,128)(2,1)}), bf16[512,5376]{0,1:T(8,128)(2,1)}) %all-gather.14.cloned.1.call-update) | async-done | bytes 5505040 | tf_op jit(solution)/shard_map/all_gather | solution.py:118
  363.9 7.5 %convolution_convert_fusion = bf16[512,5376]{1,0:T(8,128)(2,1)} fusion(bf16[512,512]{0,1:T(8,128)(2,1)S(1)} %bitcast.68, bf16[512,5376]{0,1:T(8,128)(2,1)} %all-gather.14.cloned.1.call-done), kind=kOutput, calls=%fused_computation.9 | convolution fusion | flops 2821324800 | bytes 11534336 | tf_op jit(solution)/shard_map/dot_general | solution.py:116
  371.4 0.0 copy-start
  371.4 0.0 copy-start.2
  371.4 0.0 reduce-scatter.2.cloned.1.call-update
  371.4 51.3 %reduce-scatter.2.cloned.1.call-done = bf16[128,5376]{1,0:T(8,128)(2,1)} async-done(((bf16[512,5376]{1,0:T(8,128)(2,1)}), bf16[128,5376]{1,0:T(8,128)(2,1)}) %reduce-scatter.2.cloned.1.call-update) | async-done | bytes 1376272 | tf_op jit(solution)/shard_map/reduce_scatter | solution.py:121
  422.7 1.7 fusion.12
  424.4 0.0 copy-done
  424.4 0.0 copy-done.2
  424.4 3.0 fusion.15
  (6 shorter events, 0.1 us)
Async XLA Ops:
  6.5 105.2 %copy-start.5 = (f32[5376]{0:T(1024)S(1)}, f32[5376]{0:T(1024)}, u32[]{:S(2)}) copy-start(f32[5376]{0:T(1024)} %param.16) | copy-start | bytes 64516
  6.5 47.0 %all-gather.6.cloned.1.call-start = ((), (), s32[]{:S(2)}) async-start(), calls=%async_computation.1 | async-start | bytes 6881280 | tf_op jit(solution)/shard_map/all_gather | solution.py:73
  7.3 104.5 %all-gather.8.cloned.1.call-start = ((), (), s32[]{:S(2)}) async-start(), calls=%async_computation.2 | async-start | bytes 3096576 | tf_op jit(solution)/shard_map/all_gather | solution.py:84
  8.0 160.6 %all-gather.10.cloned.1.call-start = ((), (), s32[]{:S(2)}) async-start(), calls=%async_computation.3 | async-start | bytes 3096576 | tf_op jit(solution)/shard_map/all_gather | solution.py:85
  8.7 265.8 %all-gather.12.cloned.1.call-start = ((), (), s32[]{:S(2)}) async-start(), calls=%async_computation.4 | async-start | bytes 6193152 | tf_op jit(solution)/shard_map/all_gather | solution.py:83
  9.3 354.5 %all-gather.14.cloned.1.call-start = ((), (), s32[]{:S(2)}) async-start(), calls=%async_computation.5 | async-start | bytes 6193152 | tf_op jit(solution)/shard_map/all_gather | solution.py:118
  9.9 412.8 %reduce-scatter.2.cloned.1.call-start = ((), (), s32[]{:S(2)}) async-start(), calls=%async_computation.6 | async-start | bytes 6881280 | tf_op jit(solution)/shard_map/reduce_scatter | solution.py:121
  117.4 56.8 %copy-start.3 = (f32[128]{0:T(128)S(1)}, f32[128]{0:T(128)}, u32[]{:S(2)}) copy-start(f32[128]{0:T(128)} %param.18) | copy-start | bytes 1540
  174.8 19.4 %collective-permute-start = (bf16[2,512,2,128]{3,1,2,0:T(8,128)(2,1)S(1)}, bf16[2,512,2,128]{3,1,2,0:T(8,128)(2,1)S(1)}, u32[]{:S(2)}, u32[]{:S(2)}) collective-permute-start(bf16[2,512,2,128]{3,1,2,0:T(8,128)(2,1)S(1)} %pad_maximum_fusion), channel_id=1, source_target_pairs={{0,4},{4,8},{8,12},{12,16},{16,20},{20,24},{24,28},{1,5},{5,9},{9,... | collective-permute-start | bytes 1572872 | tf_op jit(solution)/shard_map/ppermute | solution.py:16
  194.2 10.4 %copy-start.1 = (bf16[2,512,2,128]{3,1,2,0:T(8,128)(2,1)}, bf16[2,512,2,128]{3,1,2,0:T(8,128)(2,1)S(1)}, u32[]{:S(2)}) copy-start(bf16[2,512,2,128]{3,1,2,0:T(8,128)(2,1)S(1)} %collective-permute-done) | copy-start | bytes 1572868
  194.2 15.5 %collective-permute-start.1 = (bf16[2,512,2,128]{3,1,2,0:T(8,128)(2,1)S(1)}, bf16[2,512,2,128]{3,1,2,0:T(8,128)(2,1)S(1)}, u32[]{:S(2)}, u32[]{:S(2)}) collective-permute-start(bf16[2,512,2,128]{3,1,2,0:T(8,128)(2,1)S(1)} %collective-permute-done), channel_id=1, source_target_pairs={{0,4},{4,8},{8,12},{12,16},{16,20},{20,24},{24,28},{1,5},{5,9},{9,... | collective-permute-start | bytes 1572872 | tf_op jit(solution)/shard_map/ppermute | solution.py:16
  211.0 71.6 %copy-start.4 = (f32[128]{0:T(128)S(1)}, f32[128]{0:T(128)}, u32[]{:S(2)}) copy-start(f32[128]{0:T(128)} %param.17) | copy-start | bytes 1540
  371.4 53.0 %copy-start = (bf16[128,5376]{1,0:T(8,128)(2,1)S(1)}, bf16[128,5376]{1,0:T(8,128)(2,1)}, u32[]{:S(2)}) copy-start(bf16[128,5376]{1,0:T(8,128)(2,1)} %param.10) | copy-start | bytes 4128772
  371.4 53.1 %copy-start.2 = (f32[5376]{0:T(1024)S(1)}, f32[5376]{0:T(1024)}, u32[]{:S(2)}) copy-start(f32[5376]{0:T(1024)} %param.19) | copy-start | bytes 64516
Sparse Core Ops, SparseCore 0:
  8.9 44.6 all-gather.5
  55.7 55.9 all-gather.7
  114.0 54.5 all-gather.9
  170.6 103.8 all-gather.11
  276.6 87.2 all-gather.13
  371.5 51.1 reduce-scatter.1
where the time goes:
time: 435 us; the launch traced here: 434 us
  waiting for transfers between devices  353 us (81%)
  matrix products  39.2 us (9%)
  other arithmetic  13.9 us (3%)
  between operations  13.7 us (3%)
  starting transfers between devices  11.8 us (3%)
    all_gather x1, waiting for transfers between devices, shards(): lax.all_gather(w_out, 'ctx', axis=1, tiled=True)  66.7 us
    all_gather x1, waiting for transfers between devices, shards(): query_raw = add_rows(lax.all_gather(w_query, 'ctx', axis=0, tiled=True))  63.6 us
    all_gather x1, waiting for transfers between devices, shards(): lax.all_gather(key_matrix, 'ctx', axis=0, tiled=True)  54.5 us
    reduce_scatter x1, waiting for transfers between devices, shards(): lax.psum_scatter(projected.astype(jnp.bfloat16), 'tp', scatter_dimension=...  51.3 us
    all_gather x1, waiting for transfers between devices, shards(): lax.all_gather(value_matrix, 'ctx', axis=0, tiled=True)  51.2 us
    all_gather x1, waiting for transfers between devices, shards(): gathered = lax.all_gather(tokens, 'tp', axis=0, tiled=True)  40.1 us
    ppermute x2, waiting for transfers between devices, shifted(): lax.ppermute(value, axis, [(source, source + steps) for source in range(l...  22 us
    dot_general x3, matrix products, add_rows(): jnp.dot(normalized_rows, weight_rows, preferred_element_type=jnp.float32)  18.8 us
  transfers between devices with their start and end apart: 8, of which 8 were waited for; matrix products, arithmetic and copies ran while one was open for 10% of the time, Pallas kernels for 0%

commit v1 on v0

--- a/solution.py
+++ b/solution.py
@@ -80,7 +80,11 @@
     def add_rows(weight_rows):
         return jnp.dot(normalized_rows, weight_rows, preferred_element_type=jnp.float32)
 
-    query_raw = add_rows(lax.all_gather(w_query, "ctx", axis=0, tiled=True))
+    query_raw = add_rows(
+        jnp.concatenate(
+            lax.all_to_all(jnp.stack([w_query] * lax.axis_size("ctx")), "ctx", 0, 0), axis=0
+        )
+    )
     unnormed_keys = add_rows(lax.all_gather(key_matrix, "ctx", axis=0, tiled=True))
     value_raw = add_rows(lax.all_gather(value_matrix, "ctx", axis=0, tiled=True))
     key_heads = key_matrix.shape[1] // HEAD_SIZE

time: 435 us -> 410 us (0.943)
  waiting for transfers between devices: 353 us -> 311 us
  local copies, waits for them, and re-layouts: 3.21 us -> 14.8 us
  starting transfers between devices: 11.8 us -> 19.1 us
    all_gather x1, waiting for transfers between devices: 54.5 us -> 119 us  [shards(): lax.all_gather(key_matrix, 'ctx', axis=0, tiled=True)]
    all_gather x1 -> x0, waiting for transfers between devices: 63.6 us -> none  [shards(): query_raw = add_rows(lax.all_gather(w_query, 'ctx', axis=0, tiled=True))]
    all_gather x1, waiting for transfers between devices: 66.7 us -> 33.8 us  [shards(): lax.all_gather(w_out, 'ctx', axis=1, tiled=True)]
    all_gather x1, waiting for transfers between devices: 40.1 us -> 30.7 us  [shards(): gathered = lax.all_gather(tokens, 'tp', axis=0, tiled=True)]
    dot_general x0 -> x1, local copies, waits for them, and re-layouts: none -> 8.31 us  [add_rows(): jnp.dot(normalized_rows, weight_rows, preferred_element_type=jnp.float32)]
    all_to_all x0 -> x1, starting transfers between devices: none -> 7.44 us  [shards(): lax.all_to_all(jnp.stack([w_query] * lax.axis_size('ctx')), 'ctx', 0, 0)]
  transfers between devices with their start and end apart: 8 -> 8, of which waited for: 8 -> 7; matrix products, arithmetic and copies ran while one was open for 10% -> 13% of each run, Pallas kernels for 0% -> 0%
where the time goes in v1:
time: 410 us; the launch traced here: 409 us
  waiting for transfers between devices  311 us (76%)
  matrix products  38 us (9%)
  starting transfers between devices  19.1 us (5%)
  local copies, waits for them, and re-layouts  14.8 us (4%)
  between operations  13.4 us (3%)
  other arithmetic  13.2 us (3%)
    all_gather x1, waiting for transfers between devices, shards(): lax.all_gather(key_matrix, 'ctx', axis=0, tiled=True)  119 us
    reduce_scatter x1, waiting for transfers between devices, shards(): lax.psum_scatter(projected.astype(jnp.bfloat16), 'tp', scatter_dimension=...  51.3 us
    all_gather x1, waiting for transfers between devices, shards(): lax.all_gather(value_matrix, 'ctx', axis=0, tiled=True)  50.9 us
    all_gather x1, waiting for transfers between devices, shards(): lax.all_gather(w_out, 'ctx', axis=1, tiled=True)  33.8 us
    all_gather x1, waiting for transfers between devices, shards(): gathered = lax.all_gather(tokens, 'tp', axis=0, tiled=True)  30.7 us
    ppermute x2, waiting for transfers between devices, shifted(): lax.ppermute(value, axis, [(source, source + steps) for source in range(l...  22 us
    dot_general x3, matrix products, add_rows(): jnp.dot(normalized_rows, weight_rows, preferred_element_type=jnp.float32)  17.6 us
    ppermute x2, starting transfers between devices, shifted(): lax.ppermute(value, axis, [(source, source + steps) for source in range(l...  11.5 us
  transfers between devices with their start and end apart: 8, of which 7 were waited for; matrix products, arithmetic and copies ran while one was open for 13% of the time, Pallas kernels for 0%

profile of v1, /device:TPU:0, one launch (start us, length us, event | category | flops | bytes accessed | tf_op | source)
XLA Modules:
  0.0 409.2 jit_solution(415485943000765825)
XLA Ops:
  6.5 0.0 all-gather.5.cloned.1.call-start
  6.5 0.7 all-gather.5.cloned.1.call-update
  7.3 0.0 all-gather.7.cloned.1.call-start
  7.3 0.7 all-gather.7.cloned.1.call-update
  8.0 0.0 all-gather.9.cloned.1.call-start
  8.1 0.7 all-gather.9.cloned.1.call-update
  8.7 4.0 stack.5
  12.7 0.0 copy-start.3
  12.7 7.4 %all-to-all-start = ((bf16[8,672,512]{2,1,0:T(8,128)(2,1)}), bf16[8,672,512]{2,1,0:T(8,128)(2,1)}, u32[]{:S(2)}, u32[]{:S(2)}) async-start(bf16[8,672,512]{2,1,0:T(8,128)(2,1)} %stack.5), calls=%async_computation | async-start | bytes 11010048 | tf_op jit(solution)/shard_map/all_to_all | solution.py:85
  20.1 0.0 copy-start.6
  20.1 0.0 all-gather.11.cloned.1.call-start
  20.2 0.5 all-gather.11.cloned.1.call-update
  20.7 0.0 reduce-scatter.2.cloned.1.call-start
  20.8 0.0 copy-done.3
  20.8 0.5 slice.22
  21.3 0.7 broadcast_subtract_fusion
  22.0 0.1 fusion.42
  22.1 0.5 multiply_cosine_fusion
  22.6 0.1 copy.21
  22.7 0.1 copy.22
  22.9 30.7 %all-gather.5.cloned.1.call-done = bf16[512,5376]{1,0:T(8,128)(2,1)} async-done(((bf16[128,5376]{1,0:T(8,128)(2,1)}), bf16[512,5376]{1,0:T(8,128)(2,1)}) %all-gather.5.cloned.1.call-update) | async-done | bytes 5505040 | tf_op jit(solution)/shard_map/all_gather | solution.py:73
  53.5 3.7 fusion.1
  57.3 119.4 %all-gather.7.cloned.1.call-done = bf16[5376,256]{1,0:T(8,128)(2,1)} async-done(((bf16[672,256]{1,0:T(8,128)(2,1)}), bf16[5376,256]{1,0:T(8,128)(2,1)}) %all-gather.7.cloned.1.call-update) | async-done | bytes 2752528 | tf_op jit(solution)/shard_map/all_gather | solution.py:88
  176.7 0.0 copy-done.6
  176.7 5.4 %multiply_reduce_fusion.1 = (f32[512,2]{0,1:T(2,128)S(1)}, f32[512,256]{0,1:T(8,128)S(1)}) fusion(bf16[5376,256]{1,0:T(8,128)(2,1)} %all-gather.7.cloned.1.call-done, bf16[512,5376]{1,0:T(8,128)(2,1)} %all-gather.5.cloned.1.call-done, f32[5376]{0:T(1024)S(1)} %copy-done.6, f32[512]{0:T(512)S(1)} %add_rsqrt_fusion.2), kind=kOutput, calls=%fused_computation.45 | convolution fusion | flops 1420557312 | bytes 8809472 | tf_op jit(solution)/shard_map/dot_general | solution.py:81
  182.1 0.2 copy.20
  182.3 0.0 copy-start.4
  182.3 50.9 %all-gather.9.cloned.1.call-done = bf16[5376,256]{1,0:T(8,128)(2,1)} async-done(((bf16[672,256]{1,0:T(8,128)(2,1)}), bf16[5376,256]{1,0:T(8,128)(2,1)}) %all-gather.9.cloned.1.call-update) | async-done | bytes 2752528 | tf_op jit(solution)/shard_map/all_gather | solution.py:89
  233.2 5.4 %convolution_convert_fusion.1 = bf16[512,256]{0,1:T(8,128)(2,1)S(1)} fusion(bf16[5376,256]{1,0:T(8,128)(2,1)} %all-gather.9.cloned.1.call-done, bf16[512,5376]{1,0:T(8,128)(2,1)} %all-gather.5.cloned.1.call-done, f32[5376]{0:T(1024)S(1)} %copy-done.6, f32[512]{0:T(512)S(1)} %add_rsqrt_fusion.2), kind=kOutput, calls=%fused_computation.32 | convolution fusion | flops 1420427264 | bytes 8543232 | tf_op jit(solution)/shard_map/dot_general | solution.py:81
  238.6 0.2 copy.23
  238.8 0.0 copy-done.4
  238.8 0.2 multiply_multiply_fusion.1
  239.0 0.2 fusion.30
  239.3 0.2 pad_maximum_fusion
  239.4 2.5 collective-permute-start
  241.9 0.1 pad_dynamic-slice_fusion
  242.0 16.8 %collective-permute-done = bf16[2,512,2,128]{3,1,2,0:T(8,128)(2,1)S(1)} collective-permute-done((bf16[2,512,2,128]{3,1,2,0:T(8,128)(2,1)S(1)}, bf16[2,512,2,128]{3,1,2,0:T(8,128)(2,1)S(1)}, u32[]{:S(2)}, u32[]{:S(2)}) %collective-permute-start) | collective-permute-done | bytes 524320 | tf_op jit(solution)/shard_map/ppermute | solution.py:16
  258.8 0.0 copy-start.1
  258.8 9.0 %collective-permute-start.1 = (bf16[2,512,2,128]{3,1,2,0:T(8,128)(2,1)S(1)}, bf16[2,512,2,128]{3,1,2,0:T(8,128)(2,1)S(1)}, u32[]{:S(2)}, u32[]{:S(2)}) collective-permute-start(bf16[2,512,2,128]{3,1,2,0:T(8,128)(2,1)S(1)} %collective-permute-done), channel_id=1, source_target_pairs={{0,4},{4,8},{8,12},{12,16},{16,20},{20,24},{24,28},{1,5},{5,9},{9,... | collective-permute-start | bytes 1572872 | tf_op jit(solution)/shard_map/ppermute | solution.py:16
  267.9 1.3 fusion.13
  269.1 0.0 copy-done.1
  269.1 5.2 %collective-permute-done.1 = bf16[2,512,2,128]{3,1,2,0:T(8,128)(2,1)S(1)} collective-permute-done((bf16[2,512,2,128]{3,1,2,0:T(8,128)(2,1)S(1)}, bf16[2,512,2,128]{3,1,2,0:T(8,128)(2,1)S(1)}, u32[]{:S(2)}, u32[]{:S(2)}) %collective-permute-start.1) | collective-permute-done | bytes 524320 | tf_op jit(solution)/shard_map/ppermute | solution.py:16
  274.3 1.2 maximum_maximum_fusion
  275.6 0.0 all-to-all-done
  275.6 8.3 %copy.24 = bf16[512,5376]{1,0:T(8,128)(2,1)} copy(bf16[512,5376]{0,1:T(8,128)(2,1)} %bitcast.12) | data formatting | bytes 11010048 | tf_op jit(solution)/shard_map/dot_general | solution.py:81
  283.9 0.0 copy-start.5
  283.9 6.9 %multiply_reduce_fusion = (f32[512,4]{0,1:T(4,128)S(1)}, f32[512,4,128]{0,2,1:T(8,128)S(1)}) fusion(bf16[4,128,5376]{2,1,0:T(8,128)(2,1)} %bitcast.70, f32[5376]{0:T(1024)S(1)} %copy-done.6, f32[512]{0:T(512)S(1)} %add_rsqrt_fusion.2, bf16[512,5376]{1,0:T(8,128)(2,1)} %all-gather.5.cloned.1.call-done), kind=kOutput, calls=%fused_computation.34 | convolution fusion | flops 2830104576 | bytes 12090368 | tf_op jit(solution)/shard_map/dot_general | solution.py:81
  290.8 0.0 copy-done.5
  290.8 0.2 multiply_multiply_fusion
  291.0 0.2 subtract_convert_fusion
  291.2 1.0 copy.25
  292.2 0.3 copy.26
  292.5 9.0 %fusion.43 = (f32[2,2,512]{2,1,0:T(2,128)S(1)}, bf16[2,2,512,1536]{2,3,1,0:T(8,128)(2,1)}) fusion(pred[512,1536]{0,1:T(8,128)(4,1)S(1)} %fusion.13, bf16[2,1536,2,128]{3,1,2,0:T(8,128)(2,1)S(1)} %maximum_maximum_fusion, bf16[512,2,2,64]{3,0,2,1:T(8,128)(2,1)S(1)} %copy.26, bf16[512,2,2,64]{3,0,2,1:T(8,128)(2,1)} %copy.25), kind=kOutput, calls=%fused_computation.64 | convolution fusion | flops 825230848 | bytes 9183232 | tf_op jit(solution)/shard_map/sub | solution.py:51
  301.5 3.8 fusion.26
  305.3 33.8 %all-gather.11.cloned.1.call-done = bf16[512,5376]{0,1:T(8,128)(2,1)} async-done(((bf16[512,672]{0,1:T(8,128)(2,1)}), bf16[512,5376]{0,1:T(8,128)(2,1)}) %all-gather.11.cloned.1.call-update) | async-done | bytes 5505040 | tf_op jit(solution)/shard_map/all_gather | solution.py:122
  339.1 7.5 %convolution_convert_fusion = bf16[512,5376]{1,0:T(8,128)(2,1)} fusion(bf16[512,512]{0,1:T(8,128)(2,1)S(1)} %bitcast.75, bf16[512,5376]{0,1:T(8,128)(2,1)} %all-gather.11.cloned.1.call-done), kind=kOutput, calls=%fused_computation.9 | convolution fusion | flops 2821324800 | bytes 11534336 | tf_op jit(solution)/shard_map/dot_general | solution.py:120
  346.6 0.0 copy-start
  346.6 0.0 copy-start.2
  346.6 0.0 reduce-scatter.2.cloned.1.call-update
  346.7 51.3 %reduce-scatter.2.cloned.1.call-done = bf16[128,5376]{1,0:T(8,128)(2,1)} async-done(((bf16[512,5376]{1,0:T(8,128)(2,1)}), bf16[128,5376]{1,0:T(8,128)(2,1)}) %reduce-scatter.2.cloned.1.call-update) | async-done | bytes 1376272 | tf_op jit(solution)/shard_map/reduce_scatter | solution.py:125
  398.0 1.7 fusion.14
  399.7 0.0 copy-done
  399.7 0.0 copy-done.2
  399.7 3.0 fusion.17
  (6 shorter events, 0.1 us)
Async XLA Ops:
  6.5 47.0 %all-gather.5.cloned.1.call-start = ((), (), s32[]{:S(2)}) async-start(), calls=%async_computation.2 | async-start | bytes 6881280 | tf_op jit(solution)/shard_map/all_gather | solution.py:73
  7.3 169.4 %all-gather.7.cloned.1.call-start = ((), (), s32[]{:S(2)}) async-start(), calls=%async_computation.3 | async-start | bytes 3096576 | tf_op jit(solution)/shard_map/all_gather | solution.py:88
  8.0 225.2 %all-gather.9.cloned.1.call-start = ((), (), s32[]{:S(2)}) async-start(), calls=%async_computation.4 | async-start | bytes 3096576 | tf_op jit(solution)/shard_map/all_gather | solution.py:89
  12.7 8.1 %copy-start.3 = (s32[4096]{0:T(1024)S(1)}, s32[4096]{0:T(1024)}, u32[]{:S(2)}) copy-start(s32[4096]{0:T(1024)} %param.11) | copy-start | bytes 49156
  12.7 262.9 %all-to-all-start = ((bf16[8,672,512]{2,1,0:T(8,128)(2,1)}), bf16[8,672,512]{2,1,0:T(8,128)(2,1)}, u32[]{:S(2)}, u32[]{:S(2)}) async-start(bf16[8,672,512]{2,1,0:T(8,128)(2,1)} %stack.5), calls=%async_computation | async-start | bytes 11010048 | tf_op jit(solution)/shard_map/all_to_all | solution.py:85
  20.1 156.5 %copy-start.6 = (f32[5376]{0:T(1024)S(1)}, f32[5376]{0:T(1024)}, u32[]{:S(2)}) copy-start(f32[5376]{0:T(1024)} %param.16) | copy-start | bytes 64516
  20.1 319.0 %all-gather.11.cloned.1.call-start = ((), (), s32[]{:S(2)}) async-start(), calls=%async_computation.5 | async-start | bytes 6193152 | tf_op jit(solution)/shard_map/all_gather | solution.py:122
  20.7 377.3 %reduce-scatter.2.cloned.1.call-start = ((), (), s32[]{:S(2)}) async-start(), calls=%async_computation.6 | async-start | bytes 6881280 | tf_op jit(solution)/shard_map/reduce_scatter | solution.py:125
  182.3 56.5 %copy-start.4 = (f32[128]{0:T(128)S(1)}, f32[128]{0:T(128)}, u32[]{:S(2)}) copy-start(f32[128]{0:T(128)} %param.18) | copy-start | bytes 1540
  239.4 19.4 %collective-permute-start = (bf16[2,512,2,128]{3,1,2,0:T(8,128)(2,1)S(1)}, bf16[2,512,2,128]{3,1,2,0:T(8,128)(2,1)S(1)}, u32[]{:S(2)}, u32[]{:S(2)}) collective-permute-start(bf16[2,512,2,128]{3,1,2,0:T(8,128)(2,1)S(1)} %pad_maximum_fusion), channel_id=1, source_target_pairs={{0,4},{4,8},{8,12},{12,16},{16,20},{20,24},{24,28},{1,5},{5,9},{9,... | collective-permute-start | bytes 1572872 | tf_op jit(solution)/shard_map/ppermute | solution.py:16
  258.8 10.3 %copy-start.1 = (bf16[2,512,2,128]{3,1,2,0:T(8,128)(2,1)}, bf16[2,512,2,128]{3,1,2,0:T(8,128)(2,1)S(1)}, u32[]{:S(2)}) copy-start(bf16[2,512,2,128]{3,1,2,0:T(8,128)(2,1)S(1)} %collective-permute-done) | copy-start | bytes 1572868
  258.8 15.5 %collective-permute-start.1 = (bf16[2,512,2,128]{3,1,2,0:T(8,128)(2,1)S(1)}, bf16[2,512,2,128]{3,1,2,0:T(8,128)(2,1)S(1)}, u32[]{:S(2)}, u32[]{:S(2)}) collective-permute-start(bf16[2,512,2,128]{3,1,2,0:T(8,128)(2,1)S(1)} %collective-permute-done), channel_id=1, source_target_pairs={{0,4},{4,8},{8,12},{12,16},{16,20},{20,24},{24,28},{1,5},{5,9},{9,... | collective-permute-start | bytes 1572872 | tf_op jit(solution)/shard_map/ppermute | solution.py:16
  283.9 6.9 %copy-start.5 = (f32[128]{0:T(128)S(1)}, f32[128]{0:T(128)}, u32[]{:S(2)}) copy-start(f32[128]{0:T(128)} %param.17) | copy-start | bytes 1540
  346.6 53.0 %copy-start = (bf16[128,5376]{1,0:T(8,128)(2,1)S(1)}, bf16[128,5376]{1,0:T(8,128)(2,1)}, u32[]{:S(2)}) copy-start(bf16[128,5376]{1,0:T(8,128)(2,1)} %param.10) | copy-start | bytes 4128772
  346.6 53.1 %copy-start.2 = (f32[5376]{0:T(1024)S(1)}, f32[5376]{0:T(1024)}, u32[]{:S(2)}) copy-start(f32[5376]{0:T(1024)} %param.19) | copy-start | bytes 64516
Sparse Core Ops, SparseCore 0:
  8.9 44.6 all-gather.4
  55.7 120.9 all-gather.6
  178.9 54.2 all-gather.8
  235.2 103.8 all-gather.10
  346.8 51.1 reduce-scatter.1
